TPU v7x, 32 devices: a whole 2x2x4 slice. The times are simulated.
32 devices in a mesh: groups: 2 (over x), pass: 2 (over core), mp: 8 (over z, y).
Axes of the slice: x: 2, y: 2, z: 4, core: 2. Of those that a mesh axis runs over, the one named last changes fastest.
Arguments:
- passages: bfloat16 [4096, 1024], P(('groups', 'pass', 'mp')), parts along dimension 0, may hold values from -6 to 6
- gain: float32 [1024], replicated, may hold values from 0.1 to 1.9
- w_in: bfloat16 [1024, 65536], P(None, 'mp'), may hold values from -0.1875 to 0.1875
- w_out: bfloat16 [65536, 1024], P('mp'), may hold values from -0.0234375 to 0.0234375
- w_key: bfloat16 [1024, 16384], P(None, 'mp'), may hold values from -0.1875 to 0.1875
- w_value: bfloat16 [1024, 16384], P(None, 'mp'), may hold values from -0.1875 to 0.1875
- queries: bfloat16 [32, 256, 16384], P(('groups', 'pass'), None, 'mp'), parts along dimension 0, may hold values from -72 to 72
- ids: int32 [4096], P('groups'), parts along dimension 0, may hold values from 0 to 4094, as said below
- counts: int32 [32], P(('groups', 'pass')), parts along dimension 0, may hold values from 1 to 255, as said below
Outputs:
- context: bfloat16 [32, 256, 16384], P(('groups', 'pass'), None, 'mp'), parts along dimension 0
There are 2 independent parts, one for each index of `groups`. A program takes and returns all parts, laid end to end along the dimension named above; an argument that names none is the same for every part. Nothing has to cross between parts.
Inputs may be any that keep to these rules, and one draw needn't show every extreme that they name: counts sum to 2048; the last question has exactly 255 passages and some question exactly 1. ids are distinct; ids[r] // 256 is a question q with ids[r] % 256 < counts[q], and every such slot is named by exactly one row.
All inputs are finite; a program needn't handle non-finite values.
Results may differ from a plain program's by a relative error of at most 0.02.
The roundings to bfloat16 on the way count: a program that leaves them out, or rounds other values in their place, can miss the bound.
Values may be sent and summed in bfloat16 or wider, within the bound.
A program may use at most 192 MiB of HBM per device.

v0:
```python
import jax
import jax.numpy as jnp
from jax import lax
from jax.sharding import PartitionSpec as P

HEAD = 128
QUERIES = 256
SLOTS = 256


def feed_forward(row_block, gain, w_in, w_out):
    wide = row_block.astype(jnp.float32)
    scale = lax.rsqrt(jnp.mean(wide * wide, axis=-1, keepdims=True) + 1e-06)
    normed = (wide * scale * gain).astype(jnp.bfloat16)
    hidden = jax.nn.relu(jnp.dot(normed, w_in, preferred_element_type=jnp.float32)).astype(
        jnp.bfloat16
    )
    return jnp.dot(hidden, w_out, preferred_element_type=jnp.float32)


def per_device(passages, gain, w_in, w_out, w_key, w_value, queries, ids, counts):
    gathered = lax.all_gather(passages, "mp", axis=0, tiled=True)
    own_share = lax.psum_scatter(
        feed_forward(gathered, gain, w_in, w_out), "mp", scatter_dimension=0, tiled=True
    )
    own_rows = (passages.astype(jnp.float32) + own_share).astype(jnp.bfloat16)
    encoded = lax.all_gather(own_rows, "mp", axis=0, tiled=True)
    local_questions = counts.shape[0]
    model_width = passages.shape[1]
    slot_total = local_questions * SLOTS
    all_rows = lax.all_gather(encoded, "pass", axis=0, tiled=True)
    shifted = ids - lax.axis_index("pass") * slot_total
    inside = (shifted >= 0) & (shifted < slot_total)
    target = jnp.where(inside, shifted, slot_total)
    slot_rows = (
        jnp.zeros((slot_total, model_width), jnp.bfloat16).at[target].set(all_rows, mode="drop")
    )
    key_rows = jnp.dot(slot_rows, w_key, preferred_element_type=jnp.float32).astype(jnp.bfloat16)
    value_rows = jnp.dot(slot_rows, w_value, preferred_element_type=jnp.float32).astype(
        jnp.bfloat16
    )
    local_heads = w_key.shape[1] // HEAD
    keyed = key_rows.reshape(local_questions, SLOTS, local_heads, HEAD)
    valued = value_rows.reshape(local_questions, SLOTS, local_heads, HEAD)
    asked = queries.reshape(local_questions, QUERIES, local_heads, HEAD)
    scores = jnp.einsum("qihd,qjhd->qhij", asked, keyed, preferred_element_type=jnp.float32)
    position = jnp.arange(SLOTS, dtype=jnp.int32)
    valid_key = position[None, None, None, :] < counts[:, None, None, None]
    scores = jnp.where(valid_key, scores, -1e30)
    peak = jnp.max(scores, axis=-1, keepdims=True)
    raised = jnp.where(valid_key, jnp.exp(scores - peak), 0.0)
    weights = (raised / jnp.sum(raised, axis=-1, keepdims=True)).astype(jnp.bfloat16)
    mixed = jnp.einsum("qhij,qjhd->qihd", weights, valued, preferred_element_type=jnp.float32)
    return mixed.reshape(local_questions, QUERIES, local_heads * HEAD).astype(jnp.bfloat16)


def solution(mesh):
    placed = (
        P(("groups", "pass", "mp"), None),
        P(),
        P(None, "mp"),
        P("mp", None),
        P(None, "mp"),
        P(None, "mp"),
        P(("groups", "pass"), None, "mp"),
        P("groups"),
        P(("groups", "pass")),
    )
    return jax.shard_map(
        per_device,
        mesh=mesh,
        in_specs=placed,
        out_specs=P(("groups", "pass"), None, "mp"),
        check_vma=False,
    )
```

profile of v0, /device:TPU:0, one launch (start us, length us, event | category | flops | bytes accessed | tf_op | source)
XLA Modules:
  0.0 415.7 jit_solution(15696875548011298462)
XLA Ops:
  6.5 0.7 all-gather.4.cloned.1.call-update
  7.3 0.0 reduce-scatter.2.cloned.1.call-start
  7.3 54.0 %all-gather.4.cloned.1.call-done = bf16[1024,1024]{1,0:T(8,128)(2,1)} async-done(((bf16[128,1024]{1,0:T(8,128)(2,1)}), bf16[1024,1024]{1,0:T(8,128)(2,1)}) %all-gather.4.cloned.1.call-update) | async-done | bytes 2097168 | tf_op jit(solution)/shard_map/all_gather | solution.py:22
  61.3 2.1 fusion.18
  63.4 26.8 %maximum_convert_fusion.clone.4 = bf16[1024,8192]{1,0:T(8,128)(2,1)} fusion(bf16[1024,8192]{1,0:T(8,128)(2,1)} %param.11, bf16[1024,1024]{1,0:T(8,128)(2,1)} %all-gather.4.cloned.1.call-done, f32[1024]{0:T(1024)} %param.10, f32[1024]{0:T(1024)S(1)} %add_rsqrt_fusion), kind=kOutput, calls=%fused_computation.8.clone.clone.clone.1 | convolution fusion | flops 17200840704 | bytes 35659776 | tf_op jit(solution)/shard_map/dot_general | solution.py:15
  90.2 23.6 %fusion.27 = f32[1024,1024]{1,0:T(8,128)} fusion(bf16[8192,1024]{1,0:T(8,128)(2,1)} %param.12, bf16[1024,8192]{1,0:T(8,128)(2,1)} %maximum_convert_fusion.clone.4), kind=kOutput, calls=%fused_computation.30 | convolution fusion | flops 17179869184 | bytes 37748736 | tf_op jit(solution)/shard_map/dot_general | solution.py:18
  113.8 0.0 reduce-scatter.2.cloned.1.call-update
  113.8 0.0 all-gather.6.cloned.1.call-start
  113.9 86.9 %reduce-scatter.2.cloned.1.call-done = f32[128,1024]{1,0:T(8,128)} async-done(((f32[1024,1024]{1,0:T(8,128)}), f32[128,1024]{1,0:T(8,128)}) %reduce-scatter.2.cloned.1.call-update) | async-done | bytes 524304 | tf_op jit(solution)/shard_map/reduce_scatter | solution.py:23
  200.8 1.8 add_convert_fusion
  202.6 0.0 all-gather.6.cloned.1.call-update
  202.6 0.0 all-gather.8.cloned.1.call-start
  202.7 49.0 %all-gather.6.cloned.1.call-done = bf16[1024,1024]{1,0:T(8,128)(2,1)} async-done(((bf16[128,1024]{1,0:T(8,128)(2,1)}), bf16[1024,1024]{1,0:T(8,128)(2,1)}) %all-gather.6.cloned.1.call-update) | async-done | bytes 2097168 | tf_op jit(solution)/shard_map/all_gather | solution.py:27
  251.7 0.1 iota_compare_fusion
  251.8 13.5 %all-gather.8.cloned.1.call-done = bf16[2048,1024]{1,0:T(8,128)(2,1)} async-done(((bf16[1024,1024]{1,0:T(8,128)(2,1)}), bf16[2048,1024]{1,0:T(8,128)(2,1)}) %all-gather.8.cloned.1.call-update) | async-done | bytes 4194320 | tf_op jit(solution)/shard_map/all_gather | solution.py:31
  265.3 13.0 %scatter_custom_fusion = bf16[2048,1024]{1,0:T(8,128)(2,1)} fusion(s32[2048]{0:T(1024)S(1)} %compare_select_fusion, bf16[2048,1024]{1,0:T(8,128)(2,1)} %all-gather.8.cloned.1.call-done, bf16[]{:T(256)} %constant.10.clone.1), kind=kCustom, calls=%fused_computation.28 | custom fusion | bytes 4194816 | tf_op jit(solution)/shard_map/scatter | solution.py:36
  278.3 13.9 %convert_bitcast_fusion = bf16[256,8,16,128]{3,1,2,0:T(8,128)(2,1)} fusion(bf16[2048,1024]{1,0:T(8,128)(2,1)} %scatter_custom_fusion, bf16[1024,2048]{1,0:T(8,128)(2,1)} %param.13), kind=kOutput, calls=%fused_computation.18 | convolution fusion | flops 8594128896 | bytes 16777216 | tf_op jit(solution)/shard_map/dot_general | solution.py:38
  292.3 9.9 %copy.18 = bf16[256,8,16,128]{3,2,1,0:T(8,128)(2,1)} copy(bf16[256,8,16,128]{3,1,2,0:T(8,128)(2,1)} %convert_bitcast_fusion) | data formatting | bytes 16777216
  302.2 13.0 %convert_bitcast_fusion.1 = bf16[256,8,16,128]{3,1,2,0:T(8,128)(2,1)} fusion(bf16[2048,1024]{1,0:T(8,128)(2,1)S(1)} %copy-done, bf16[1024,2048]{1,0:T(8,128)(2,1)} %param.14), kind=kOutput, calls=%fused_computation.19 | convolution fusion | flops 8594128896 | bytes 16777216 | tf_op jit(solution)/shard_map/dot_general | solution.py:39
  315.2 9.7 %copy.17 = bf16[256,8,16,128]{3,2,1,0:T(8,128)(2,1)} copy(bf16[256,8,16,128]{3,1,2,0:T(8,128)(2,1)} %convert_bitcast_fusion.1) | data formatting | bytes 16777216
  324.9 16.6 %fusion.10 = f32[8,16,256,256]{3,2,1,0:T(8,128)} fusion(bf16[8,256,16,128]{3,2,1,0:T(8,128)(2,1)} %bitcast.42, bf16[8,256,2048]{2,1,0:T(8,128)(2,1)} %param.15), kind=kOutput, calls=%fused_computation.13 | convolution fusion | flops 2147483648 | bytes 50331648 | tf_op jit(solution)/shard_map/qihd,qjhd->qhij/dot_general | solution.py:46
  341.5 37.7 %fusion.31 = (f32[8,16,256]{2,1,0:T(8,128)S(1)}, f32[8,16,256,256]{2,3,1,0:T(8,128)}) fusion(f32[8,16,256,256]{3,2,1,0:T(8,128)} %fusion.10, pred[8,256]{1,0:T(8,128)(4,1)S(1)} %iota_compare_fusion), kind=kOutput, calls=%fused_computation.37 | output fusion | flops 41943296 | bytes 67241984 | tf_op jit(solution)/shard_map/sub | solution.py:51
  379.2 18.6 %fusion.15 = bf16[8,16,128,256]{3,2,1,0:T(8,128)(2,1)} fusion(f32[8,16,256,256]{2,3,1,0:T(8,128)} %get-tuple-element.6, f32[8,16,256]{2,1,0:T(8,128)S(1)} %get-tuple-element.5, bf16[8,256,16,128]{3,2,1,0:T(8,128)(2,1)} %bitcast.43), kind=kOutput, calls=%fused_computation.20 | convolution fusion | flops 2168455168 | bytes 50462720 | tf_op jit(solution)/shard_map/qhij,qjhd->qihd/dot_general | solution.py:53
  397.8 11.4 %copy.14 = bf16[8,256,2048]{2,1,0:T(8,128)(2,1)} copy(bf16[8,256,2048]{1,2,0:T(8,128)(2,1)} %bitcast.44) | data formatting | bytes 16777216 | tf_op jit(solution)/shard_map/convert_element_type | solution.py:54
  (12 shorter events, 0.0 us)
Async XLA Ops:
  6.5 54.8 %all-gather.4.cloned.1.call-start = ((), (), s32[]{:S(2)}) async-start(), calls=%async_computation.1 | async-start | bytes 2359296 | tf_op jit(solution)/shard_map/all_gather | solution.py:22
  7.3 193.5 %reduce-scatter.2.cloned.1.call-start = ((), (), s32[]{:S(2)}) async-start(), calls=%async_computation.2 | async-start | bytes 4718592 | tf_op jit(solution)/shard_map/reduce_scatter | solution.py:23
  90.2 110.6 %copy-start.1 = (bf16[128,1024]{1,0:T(8,128)(2,1)S(1)}, bf16[128,1024]{1,0:T(8,128)(2,1)}, u32[]{:S(2)}) copy-start(bf16[128,1024]{1,0:T(8,128)(2,1)} %param.9) | copy-start | bytes 786436
  90.2 161.5 %copy-start.3 = (s32[8]{0:T(128)S(1)}, s32[8]{0:T(128)}, u32[]{:S(2)}) copy-start(s32[8]{0:T(128)} %param.17) | copy-start | bytes 100
  90.2 161.6 %copy-start.2 = (s32[2048]{0:T(1024)S(1)}, s32[2048]{0:T(1024)}, u32[]{:S(2)}) copy-start(s32[2048]{0:T(1024)} %param.16) | copy-start | bytes 24580
  113.8 137.9 %all-gather.6.cloned.1.call-start = ((), (), s32[]{:S(2)}) async-start(), calls=%async_computation.3 | async-start | bytes 2359296 | tf_op jit(solution)/shard_map/all_gather | solution.py:27
  202.6 62.7 %all-gather.8.cloned.1.call-start = ((), (), s32[]{:S(2)}) async-start(), calls=%async_computation.4 | async-start | bytes 6291456 | tf_op jit(solution)/shard_map/all_gather | solution.py:31
  292.3 9.9 %copy-start = (bf16[2048,1024]{1,0:T(8,128)(2,1)S(1)}, bf16[2048,1024]{1,0:T(8,128)(2,1)}, u32[]{:S(2)}) copy-start(bf16[2048,1024]{1,0:T(8,128)(2,1)} %scatter_custom_fusion) | copy-start | bytes 12582916
Sparse Core Ops, SparseCore 0:
  9.5 51.7 all-gather.3
  113.9 86.8 reduce-scatter.1
  202.9 48.7 all-gather.5
  253.1 12.1 all-gather.7
where the time goes:
time: 416 us
  waiting for transfers between devices  204 us (49%)
  matrix products  113 us (27%)
  local copies, waits for them, and re-layouts  44.1 us (11%)
  other arithmetic  41.6 us (10%)
  between operations  13.2 us (3%)
    reduce_scatter x1, waiting for transfers between devices, per_device(): lax.psum_scatter(feed_forward(gathered, gain, w_in, w_out), 'mp', scatter...  86.9 us
    all_gather x1, waiting for transfers between devices, per_device(): gathered = lax.all_gather(passages, 'mp', axis=0, tiled=True)  54 us
    all_gather x1, waiting for transfers between devices, per_device(): encoded = lax.all_gather(own_rows, 'mp', axis=0, tiled=True)  49 us
    sub x1, other arithmetic, per_device(): raised = jnp.where(valid_key, jnp.exp(scores - peak), 0.0)  37.7 us
    dot_general x1, matrix products, feed_forward(): jnp.dot(normed, w_in, preferred_element_type=jnp.float32)  26.8 us
    dot_general x1, matrix products, feed_forward(): return jnp.dot(hidden, w_out, preferred_element_type=jnp.float32)  23.6 us
    unnamed x10, local copies, waits for them, and re-layouts  19.7 us
    dot_general x1, matrix products, per_device(): jnp.einsum('qhij,qjhd->qihd', weights, valued, preferred_element_type=jnp...  18.6 us
  transfers between devices with their start and end apart: 4, of which 4 were waited for; matrix products, arithmetic and copies ran while one was open for 0% of the time, Pallas kernels for 0%

commit v1 on v0

v1 whole, which is shorter than its diff:
```python
import functools

import jax
import jax.numpy as jnp
from jax import lax
from jax.experimental import pallas as pl
from jax.experimental.pallas import tpu as pltpu
from jax.sharding import PartitionSpec as P

HEAD = 128
QUERIES = 256
SLOTS = 256
MESH = pl.DeviceIdType.MESH
INNER = 2


def greet(targets):
    barrier = pltpu.get_barrier_semaphore()
    for target in targets:
        pl.semaphore_signal(barrier, inc=1, device_id=target, device_id_type=MESH)
    pl.semaphore_wait(barrier, len(targets))


def push(src, dst, send_sem, recv_sem, target):
    copy = pltpu.make_async_remote_copy(
        src_ref=src, dst_ref=dst, send_sem=send_sem, recv_sem=recv_sem,
        device_id=target, device_id_type=MESH,
    )
    copy.start()
    return copy


def landed(ref, send_sem, recv_sem, target):
    pltpu.make_async_remote_copy(
        src_ref=ref, dst_ref=ref, send_sem=send_sem, recv_sem=recv_sem,
        device_id=target, device_id_type=MESH,
    ).wait_recv()


def place(outer, inner):
    me = lax.axis_index("mp")
    z, y = me // inner, me % inner
    partner = {"mp": z * inner + (1 - y)}
    ahead = [(z + 1 + k) % outer for k in range(outer - 1)]
    behind = [(z + outer - 1 - k) % outer for k in range(outer - 1)]
    return z, y, partner, ahead, behind


def gather_first(outer, rows, own_ref, out_ref, local_sem, zs, zr, ys, yr):
    z, y, partner, ahead, behind = place(outer, INNER)
    greet([partner] + [{"mp": zz * INNER + y} for zz in ahead])

    def block(zz, yy):
        return out_ref.at[pl.ds(pl.multiple_of((zz * INNER + yy) * rows, rows), rows)]

    mine = block(z, y)
    sent = [push(own_ref, mine, ys.at[0], yr.at[0], partner)]
    for k in range(outer - 1):
        sent.append(push(own_ref, mine, zs.at[k], zr.at[k], {"mp": ahead[k] * INNER + y}))
    local = pltpu.make_async_copy(own_ref, mine, local_sem)
    local.start()
    for k in range(outer - 1):
        arrived = block(behind[k], y)
        landed(arrived, zs.at[k], zr.at[k], partner)
        sent.append(push(arrived, arrived, ys.at[k + 1], yr.at[k + 1], partner))
    for k in range(outer):
        zz = z if k == 0 else behind[k - 1]
        arrived = block(zz, 1 - y)
        landed(arrived, ys.at[k], yr.at[k], partner)
    for copy in sent:
        copy.wait_send()
    local.wait()


def all_gather_rows(passages, outer):
    rows, width = passages.shape
    return pl.pallas_call(
        functools.partial(gather_first, outer, rows),
        out_shape=jax.ShapeDtypeStruct((outer * INNER * rows, width), passages.dtype),
        in_specs=[pl.BlockSpec(memory_space=pltpu.VMEM)],
        out_specs=pl.BlockSpec(memory_space=pltpu.VMEM),
        scratch_shapes=[
            pltpu.SemaphoreType.DMA,
            pltpu.SemaphoreType.DMA((outer - 1,)),
            pltpu.SemaphoreType.DMA((outer - 1,)),
            pltpu.SemaphoreType.DMA((outer,)),
            pltpu.SemaphoreType.DMA((outer,)),
        ],
        compiler_params=pltpu.CompilerParams(collective_id=0, has_side_effects=True),
        name="gather_rows",
    )(passages)


def sum_and_share(
    outer, rows, part_ref, own_ref, out_ref,
    from_y, from_z, summed, rys, ryr, rzs, rzr, zs, zr, ys, yr, ps, pr,
):
    z, y, partner, ahead, behind = place(outer, INNER)
    n = outer * INNER
    p = lax.axis_index("pass")
    twin = {"pass": 1 - p}
    peers = [{"mp": zz * INNER + y} for zz in ahead]
    greet([partner, twin] + peers)

    def start(zz, yy):
        return pl.multiple_of((zz * INNER + yy) * rows, rows)

    sent = []
    order = ahead + [z]
    for k in range(outer):
        sent.append(
            push(part_ref.at[pl.ds(start(order[k], 1 - y), rows)], from_y.at[k],
                 rys.at[k], ryr.at[k], partner)
        )
    for k in range(outer - 1):
        sent[k].wait_recv()
        summed[k] = (
            part_ref[pl.ds(start(order[k], y), rows), :].astype(jnp.float32)
            + from_y[k].astype(jnp.float32)
        ).astype(jnp.bfloat16)
        sent.append(push(summed.at[k], from_z.at[k], rzs.at[k], rzr.at[k], peers[k]))
    sent[outer - 1].wait_recv()
    total = part_ref[pl.ds(start(z, y), rows), :].astype(jnp.float32) + from_y[
        outer - 1
    ].astype(jnp.float32)
    for k in range(outer - 1):
        sent[outer + k].wait_recv()
        total += from_z[k].astype(jnp.float32)
    own = pl.multiple_of(p * n * rows + start(z, y), rows)
    out_ref[pl.ds(own, rows), :] = (own_ref[...].astype(jnp.float32) + total).astype(jnp.bfloat16)

    def block(pp, zz, yy):
        return out_ref.at[pl.ds(pl.multiple_of(pp * n * rows + start(zz, yy), rows), rows)]

    mine = block(p, z, y)
    sent.append(push(mine, mine, ys.at[0], yr.at[0], partner))
    for k in range(outer - 1):
        sent.append(push(mine, mine, zs.at[k], zr.at[k], peers[k]))
    sent.append(push(mine, mine, ps.at[0], pr.at[0], twin))
    for k in range(outer):
        if k > 0:
            arrived = block(p, behind[k - 1], y)
            landed(arrived, zs.at[k - 1], zr.at[k - 1], partner)
            sent.append(push(arrived, arrived, ys.at[k], yr.at[k], partner))
            sent.append(push(arrived, arrived, ps.at[k], pr.at[k], twin))
    for k in range(outer):
        arrived = block(p, z if k == 0 else behind[k - 1], 1 - y)
        landed(arrived, ys.at[k], yr.at[k], partner)
        sent.append(push(arrived, arrived, ps.at[outer + k], pr.at[outer + k], twin))
    for k in range(2 * outer):
        kk = k % outer
        arrived = block(1 - p, z if kk == 0 else behind[kk - 1], y if k < outer else 1 - y)
        landed(arrived, ps.at[k], pr.at[k], twin)
    for copy in sent:
        copy.wait_send()


def reduce_and_share(partial, passages, outer):
    rows, width = passages.shape
    n = outer * INNER
    dma = pltpu.SemaphoreType.DMA
    return pl.pallas_call(
        functools.partial(sum_and_share, outer, rows),
        out_shape=jax.ShapeDtypeStruct((2 * n * rows, width), jnp.bfloat16),
        in_specs=[pl.BlockSpec(memory_space=pltpu.VMEM)] * 2,
        out_specs=pl.BlockSpec(memory_space=pltpu.VMEM),
        scratch_shapes=[
            pltpu.VMEM((outer, rows, width), jnp.bfloat16),
            pltpu.VMEM((outer - 1, rows, width), jnp.bfloat16),
            pltpu.VMEM((outer - 1, rows, width), jnp.bfloat16),
            dma((outer,)), dma((outer,)),
            dma((outer - 1,)), dma((outer - 1,)),
            dma((outer - 1,)), dma((outer - 1,)),
            dma((outer,)), dma((outer,)),
            dma((2 * outer,)), dma((2 * outer,)),
        ],
        compiler_params=pltpu.CompilerParams(collective_id=1, has_side_effects=True),
        name="reduce_and_share",
    )(partial, passages)


def attend_kernel(counts_ref, ids_ref, rows_ref, wk_ref, wv_ref, q_ref, o_ref, slot_ref):
    q = pl.program_id(1)

    @pl.when(pl.program_id(0) == 0)
    def _():
        total = ids_ref.shape[1]
        slot_id = lax.broadcasted_iota(jnp.int32, (SLOTS, total), 0) + q * SLOTS
        named = jnp.where(slot_id == ids_ref[...], 1.0, 0.0).astype(jnp.bfloat16)
        slot_ref[q] = jnp.dot(
            named, rows_ref[...], preferred_element_type=jnp.float32
        ).astype(jnp.bfloat16)

    slots = slot_ref[q]
    keyed = jnp.dot(slots, wk_ref[...], preferred_element_type=jnp.float32).astype(jnp.bfloat16)
    valued = jnp.dot(slots, wv_ref[...], preferred_element_type=jnp.float32).astype(jnp.bfloat16)
    valid = lax.broadcasted_iota(jnp.int32, (QUERIES, SLOTS), 1) < counts_ref[q]
    for h in range(wk_ref.shape[1] // HEAD):
        cols = slice(h * HEAD, (h + 1) * HEAD)
        scores = lax.dot_general(
            q_ref[0, :, cols], keyed[:, cols], (((1,), (1,)), ((), ())),
            preferred_element_type=jnp.float32,
        )
        scores = jnp.where(valid, scores, -1e30)
        peak = jnp.max(scores, axis=-1, keepdims=True)
        raised = jnp.where(valid, jnp.exp(scores - peak), 0.0)
        weights = (raised * (1.0 / jnp.sum(raised, axis=-1, keepdims=True))).astype(jnp.bfloat16)
        o_ref[0, :, cols] = jnp.dot(
            weights, valued[:, cols], preferred_element_type=jnp.float32
        ).astype(jnp.bfloat16)


def attend(counts, shifted, all_rows, w_key, w_value, queries):
    questions, asked, cols = queries.shape
    total, width = all_rows.shape
    step = min(cols, 8 * HEAD)
    while cols % step:
        step -= HEAD
    return pl.pallas_call(
        attend_kernel,
        out_shape=jax.ShapeDtypeStruct(queries.shape, jnp.bfloat16),
        grid_spec=pltpu.PrefetchScalarGridSpec(
            num_scalar_prefetch=1,
            grid=(cols // step, questions),
            in_specs=[
                pl.BlockSpec((1, total), lambda c, q, s: (0, 0)),
                pl.BlockSpec((total, width), lambda c, q, s: (0, 0)),
                pl.BlockSpec((width, step), lambda c, q, s: (0, c)),
                pl.BlockSpec((width, step), lambda c, q, s: (0, c)),
                pl.BlockSpec((1, asked, step), lambda c, q, s: (q, 0, c)),
            ],
            out_specs=pl.BlockSpec((1, asked, step), lambda c, q, s: (q, 0, c)),
            scratch_shapes=[pltpu.VMEM((questions, SLOTS, width), jnp.bfloat16)],
        ),
        compiler_params=pltpu.CompilerParams(vmem_limit_bytes=56 * 1024 * 1024),
        name="attend",
    )(counts, shifted, all_rows, w_key, w_value, queries)


def feed_forward(row_block, gain, w_in, w_out):
    wide = row_block.astype(jnp.float32)
    scale = lax.rsqrt(jnp.mean(wide * wide, axis=-1, keepdims=True) + 1e-06)
    normed = (wide * scale * gain).astype(jnp.bfloat16)
    hidden = jax.nn.relu(jnp.dot(normed, w_in, preferred_element_type=jnp.float32)).astype(
        jnp.bfloat16
    )
    return jnp.dot(hidden, w_out, preferred_element_type=jnp.float32).astype(jnp.bfloat16)


def per_device(devices, passages, gain, w_in, w_out, w_key, w_value, queries, ids, counts):
    outer = devices // INNER
    gathered = all_gather_rows(passages, outer)
    partial = feed_forward(gathered, gain, w_in, w_out)
    all_rows = reduce_and_share(partial, passages, outer)
    slot_total = counts.shape[0] * SLOTS
    shifted = (ids - lax.axis_index("pass") * slot_total)[None, :]
    return attend(counts, shifted, all_rows, w_key, w_value, queries)


def solution(mesh):
    placed = (
        P(("groups", "pass", "mp"), None),
        P(),
        P(None, "mp"),
        P("mp", None),
        P(None, "mp"),
        P(None, "mp"),
        P(("groups", "pass"), None, "mp"),
        P("groups"),
        P(("groups", "pass")),
    )
    return jax.shard_map(
        functools.partial(per_device, mesh.shape["mp"]),
        mesh=mesh,
        in_specs=placed,
        out_specs=P(("groups", "pass"), None, "mp"),
        check_vma=False,
    )
```

time: 416 us -> 227 us (0.55)
  the two profiles are of different devices: /device:TPU:0 before, /device:TPU:17 now
where the time goes in v1:
time: 227 us
  Pallas kernels  174 us (77%)
  matrix products  50 us (22%)
  other arithmetic  2.67 us (1%)
    pallas_call x1, Pallas kernels, reduce_and_share(): pl.pallas_call(functools.partial(sum_and_share, outer, rows), out_shape=j...  91.8 us
    pallas_call x1, Pallas kernels, attend(): pl.pallas_call(attend_kernel, out_shape=jax.ShapeDtypeStruct(queries.shap...  56.3 us
    dot_general x1, matrix products, feed_forward(): jnp.dot(normed, w_in, preferred_element_type=jnp.float32)  26.8 us
    pallas_call x1, Pallas kernels, all_gather_rows(): pl.pallas_call(functools.partial(gather_first, outer, rows), out_shape=ja...  26 us
    dot_general x1, matrix products, feed_forward(): jnp.dot(hidden, w_out, preferred_element_type=jnp.float32)  23.2 us

profile of v1, /device:TPU:17, one launch (start us, length us, event | category | flops | bytes accessed | tf_op | source)
XLA Modules:
  0.0 226.9 jit_solution(12343141547190777397)
XLA Ops:
  0.0 0.0 copy-start.1
  0.0 26.0 %gather_rows.1 = bf16[1024,1024]{1,0:T(8,128)(2,1)} custom-call(bf16[128,1024]{1,0:T(8,128)(2,1)} %own_ref.3), custom_call_target="tpu_custom_call" | custom-call | tf_op jit(solution)/shard_map/gather_rows/pallas_call | solution.py:77
  26.0 2.1 fusion
  28.1 0.0 copy-done.1
  28.1 26.8 %fusion.26 = bf16[1024,8192]{1,0:T(8,128)(2,1)} fusion(bf16[1024,8192]{1,0:T(8,128)(2,1)} %param.11, bf16[1024,1024]{1,0:T(8,128)(2,1)} %gather_rows.1, f32[1024]{0:T(1024)S(1)} %copy-done.1, f32[1024]{0:T(1024)S(1)} %add_rsqrt_fusion), kind=kOutput, calls=%bitcast_fusion.clone.1 | convolution fusion | flops 17200840704 | bytes 35659776 | tf_op jit(solution)/shard_map/dot_general | solution.py:244
  54.9 23.2 %convolution_convert_fusion.part_ref = bf16[1024,1024]{1,0:T(8,128)(2,1)} fusion(bf16[8192,1024]{1,0:T(8,128)(2,1)} %param.12, bf16[1024,8192]{1,0:T(8,128)(2,1)} %fusion.26), kind=kOutput, calls=%fused_computation.8 | convolution fusion | flops 17180917760 | bytes 35651584 | tf_op jit(solution)/shard_map/dot_general | solution.py:247
  78.1 0.0 copy-start
  78.1 91.8 %reduce_and_share.1.rows_ref = bf16[2048,1024]{1,0:T(8,128)(2,1)} custom-call(bf16[1024,1024]{1,0:T(8,128)(2,1)} %convolution_convert_fusion.part_ref, bf16[128,1024]{1,0:T(8,128)(2,1)} %own_ref.3), custom_call_target="tpu_custom_call" | custom-call | tf_op jit(solution)/shard_map/reduce_and_share/pallas_call | solution.py:162
  169.9 0.0 copy-done
  170.0 0.6 broadcast_subtract_fusion
  170.6 56.3 %attend.1 = bf16[8,256,2048]{2,1,0:T(8,128)(2,1)} custom-call(s32[8]{0:T(128)} %counts_ref.1, s32[1,2048]{1,0:T(1,128)} %bitcast.16, bf16[2048,1024]{1,0:T(8,128)(2,1)} %reduce_and_share.1.rows_ref, bf16[1024,2048]{1,0:T(8,128)(2,1)} %wk_ref.1, bf16[1024,2048]{1,0:T(8,128)(2,1)} %wv_ref.1, bf16[8,256,2048]{2,1,0:T(8,128)(2,1)} %q_ref.1), custom_call_target="tpu_custom_call" | custom-call | tf_op jit(solution)/shard_map/attend/pallas_call | solution.py:219
  (1 shorter events, 0.0 us)
Async XLA Ops:
  0.0 28.1 %copy-start.1 = (f32[1024]{0:T(1024)S(1)}, f32[1024]{0:T(1024)}, u32[]{:S(2)}) copy-start(f32[1024]{0:T(1024)} %param.10) | copy-start | bytes 12292
  78.1 91.9 %copy-start = (s32[2048]{0:T(1024)S(1)}, s32[2048]{0:T(1024)}, u32[]{:S(2)}) copy-start(s32[2048]{0:T(1024)} %param.16) | copy-start | bytes 24580

commit v2 on v1

v2 whole, which is shorter than its diff:
```python
import functools

import jax
import jax.numpy as jnp
from jax import lax
from jax.experimental import pallas as pl
from jax.experimental.pallas import tpu as pltpu
from jax.sharding import PartitionSpec as P

HEAD = 128
QUERIES = 256
SLOTS = 256
MESH = pl.DeviceIdType.MESH
INNER = 2


def greet(targets):
    barrier = pltpu.get_barrier_semaphore()
    for target in targets:
        pl.semaphore_signal(barrier, inc=1, device_id=target, device_id_type=MESH)
    pl.semaphore_wait(barrier, len(targets))


def push(src, dst, send_sem, recv_sem, target):
    copy = pltpu.make_async_remote_copy(
        src_ref=src, dst_ref=dst, send_sem=send_sem, recv_sem=recv_sem,
        device_id=target, device_id_type=MESH,
    )
    copy.start()
    return copy


def landed(ref, send_sem, recv_sem, target):
    pltpu.make_async_remote_copy(
        src_ref=ref, dst_ref=ref, send_sem=send_sem, recv_sem=recv_sem,
        device_id=target, device_id_type=MESH,
    ).wait_recv()


def gone(ref, send_sem, recv_sem, target):
    pltpu.make_async_remote_copy(
        src_ref=ref, dst_ref=ref, send_sem=send_sem, recv_sem=recv_sem,
        device_id=target, device_id_type=MESH,
    ).wait_send()


def place(outer, inner):
    me = lax.axis_index("mp")
    z, y = me // inner, me % inner
    partner = {"mp": z * inner + (1 - y)}
    ahead = [(z + 1 + k) % outer for k in range(outer - 1)]
    behind = [(z + outer - 1 - k) % outer for k in range(outer - 1)]
    return z, y, partner, ahead, behind


def encode_kernel(
    outer, rows, chunk, own_ref, gain_ref, w_in_ref, w_out_ref, out_ref,
    gathered, w_in_here, w_out_here, normed, total, parts, from_y, from_z, summed,
    in_sem, out_sem, local_sem, gzs, gzr, gys, gyr, rys, ryr, rzs, rzr, zs, zr, ys, yr, ps, pr,
):
    z, y, partner, ahead, behind = place(outer, INNER)
    n = outer * INNER
    chunks = w_in_here.shape[0]
    p = lax.axis_index("pass")
    twin = {"pass": 1 - p}

    def load_in(c):
        cols = pl.ds(pl.multiple_of(c * chunk, chunk), chunk)
        return pltpu.make_async_copy(w_in_ref.at[:, cols], w_in_here.at[c], in_sem.at[c])

    def load_out(c):
        cols = pl.ds(pl.multiple_of(c * chunk, chunk), chunk)
        return pltpu.make_async_copy(w_out_ref.at[cols, :], w_out_here.at[c], out_sem.at[c])

    for c in range(chunks):
        load_in(c).start()
        load_out(c).start()
    greet([partner, twin] + [{"mp": zz * INNER + y} for zz in ahead])

    def start(zz, yy):
        return pl.multiple_of((zz * INNER + yy) * rows, rows)

    def held(zz, yy):
        return gathered.at[pl.ds(start(zz, yy), rows)]

    push(own_ref, held(z, y), gys.at[0], gyr.at[0], partner)
    for k in range(outer - 1):
        push(own_ref, held(z, y), gzs.at[k], gzr.at[k], {"mp": ahead[k] * INNER + y})
    local = pltpu.make_async_copy(own_ref, held(z, y), local_sem)
    local.start()
    local.wait()

    def add_pair(k):
        landed(from_y.at[k], rys.at[k], ryr.at[k], partner)
        here = parts[k, pl.ds(pl.multiple_of(y * rows, rows), rows), :]
        summed[k - 1] = (
            here.astype(jnp.float32) + from_y[k].astype(jnp.float32)
        ).astype(jnp.bfloat16)
        owner = (z + outer - k) % outer
        push(summed.at[k - 1], from_z.at[k - 1], rzs.at[k - 1], rzr.at[k - 1],
             {"mp": owner * INNER + y})

    def group(k, carry):
        zz = (z + outer - k) % outer
        landed(held(zz, 1 - y), gys.at[k], gyr.at[k], partner)
        wide = gathered[pl.ds(start(zz, 0), INNER * rows), :].astype(jnp.float32)
        scale = lax.rsqrt(jnp.mean(wide * wide, axis=-1, keepdims=True) + 1e-06)
        normed[...] = (wide * scale * gain_ref[...]).astype(jnp.bfloat16)
        total[...] = jnp.zeros_like(total)

        def piece(c, carry):
            @pl.when(k == 0)
            def _():
                load_in(c).wait()
                load_out(c).wait()

            hidden = jnp.maximum(
                jnp.dot(normed[...], w_in_here[c], preferred_element_type=jnp.float32), 0.0
            ).astype(jnp.bfloat16)
            total[...] += jnp.dot(hidden, w_out_here[c], preferred_element_type=jnp.float32)

            @pl.when((c == (chunks - 1) // 2) & (k < outer - 1))
            def _():
                later = held((z + outer - k - 1) % outer, y)
                landed(later, gzs.at[k], gzr.at[k], partner)
                push(later, later, gys.at[k + 1], gyr.at[k + 1], partner)

            @pl.when((c == (chunks - 1) // 2) & (k > 1))
            def _():
                add_pair(k - 1)

            return carry

        lax.fori_loop(0, chunks, piece, 0)
        parts[k] = total[...].astype(jnp.bfloat16)
        push(parts.at[k, pl.ds(pl.multiple_of((1 - y) * rows, rows), rows)], from_y.at[k],
             rys.at[k], ryr.at[k], partner)
        return carry

    lax.fori_loop(0, outer, group, 0)
    add_pair(outer - 1)
    landed(from_y.at[0], rys.at[0], ryr.at[0], partner)
    mine = pl.ds(pl.multiple_of(y * rows, rows), rows)
    ffn = parts[0, mine, :].astype(jnp.float32) + from_y[0].astype(jnp.float32)
    for k in range(outer - 1):
        landed(from_z.at[k], rzs.at[k], rzr.at[k], partner)
        ffn += from_z[k].astype(jnp.float32)
    own = pl.multiple_of(p * n * rows + start(z, y), rows)
    out_ref[pl.ds(own, rows), :] = (own_ref[...].astype(jnp.float32) + ffn).astype(jnp.bfloat16)

    def block(pp, zz, yy):
        return out_ref.at[pl.ds(pl.multiple_of(pp * n * rows + start(zz, yy), rows), rows)]

    mine = block(p, z, y)
    sent = [push(mine, mine, ys.at[0], yr.at[0], partner)]
    for k in range(outer - 1):
        sent.append(push(mine, mine, zs.at[k], zr.at[k], {"mp": ahead[k] * INNER + y}))
    sent.append(push(mine, mine, ps.at[0], pr.at[0], twin))
    for k in range(1, outer):
        arrived = block(p, behind[k - 1], y)
        landed(arrived, zs.at[k - 1], zr.at[k - 1], partner)
        sent.append(push(arrived, arrived, ys.at[k], yr.at[k], partner))
        sent.append(push(arrived, arrived, ps.at[k], pr.at[k], twin))
    for k in range(outer):
        arrived = block(p, z if k == 0 else behind[k - 1], 1 - y)
        landed(arrived, ys.at[k], yr.at[k], partner)
        sent.append(push(arrived, arrived, ps.at[outer + k], pr.at[outer + k], twin))
    for k in range(2 * outer):
        kk = k % outer
        arrived = block(1 - p, z if kk == 0 else behind[kk - 1], y if k < outer else 1 - y)
        landed(arrived, ps.at[k], pr.at[k], twin)
    for copy in sent:
        copy.wait_send()
    for k in range(outer):
        gone(held(z, y), gys.at[k], gyr.at[k], partner)
        gone(from_y.at[k], rys.at[k], ryr.at[k], partner)
    for k in range(outer - 1):
        gone(held(z, y), gzs.at[k], gzr.at[k], partner)
        gone(summed.at[k], rzs.at[k], rzr.at[k], partner)


def encode(passages, gain, w_in, w_out, outer):
    rows, width = passages.shape
    n = outer * INNER
    units = w_in.shape[1]
    chunk = min(units, 1024)
    while units % chunk:
        chunk -= 128
    chunks = units // chunk
    dma = pltpu.SemaphoreType.DMA
    vmem = pl.BlockSpec(memory_space=pltpu.VMEM)
    hbm = pl.BlockSpec(memory_space=pl.ANY)
    bf16 = jnp.bfloat16
    return pl.pallas_call(
        functools.partial(encode_kernel, outer, rows, chunk),
        out_shape=jax.ShapeDtypeStruct((2 * n * rows, width), bf16),
        in_specs=[vmem, vmem, hbm, hbm],
        out_specs=vmem,
        scratch_shapes=[
            pltpu.VMEM((n * rows, width), bf16),
            pltpu.VMEM((chunks, width, chunk), bf16),
            pltpu.VMEM((chunks, chunk, width), bf16),
            pltpu.VMEM((INNER * rows, width), bf16),
            pltpu.VMEM((INNER * rows, width), jnp.float32),
            pltpu.VMEM((outer, INNER * rows, width), bf16),
            pltpu.VMEM((outer, rows, width), bf16),
            pltpu.VMEM((outer - 1, rows, width), bf16),
            pltpu.VMEM((outer - 1, rows, width), bf16),
            dma((chunks,)), dma((chunks,)), dma,
            dma((outer - 1,)), dma((outer - 1,)), dma((outer,)), dma((outer,)),
            dma((outer,)), dma((outer,)), dma((outer - 1,)), dma((outer - 1,)),
            dma((outer - 1,)), dma((outer - 1,)), dma((outer,)), dma((outer,)),
            dma((2 * outer,)), dma((2 * outer,)),
        ],
        compiler_params=pltpu.CompilerParams(
            collective_id=0, has_side_effects=True, vmem_limit_bytes=60 * 1024 * 1024
        ),
        name="encode",
    )(passages, gain[None, :], w_in, w_out)


def attend_kernel(counts_ref, ids_ref, rows_ref, wk_ref, wv_ref, q_ref, o_ref, slot_ref):
    q = pl.program_id(1)

    @pl.when(pl.program_id(0) == 0)
    def _():
        total = ids_ref.shape[1]
        slot_id = lax.broadcasted_iota(jnp.int32, (SLOTS, total), 0) + q * SLOTS
        named = jnp.where(slot_id == ids_ref[...], 1.0, 0.0).astype(jnp.bfloat16)
        slot_ref[q] = jnp.dot(
            named, rows_ref[...], preferred_element_type=jnp.float32
        ).astype(jnp.bfloat16)

    slots = slot_ref[q]
    keyed = jnp.dot(slots, wk_ref[...], preferred_element_type=jnp.float32).astype(jnp.bfloat16)
    valued = jnp.dot(slots, wv_ref[...], preferred_element_type=jnp.float32).astype(jnp.bfloat16)
    valid = lax.broadcasted_iota(jnp.int32, (QUERIES, SLOTS), 1) < counts_ref[q]
    for h in range(wk_ref.shape[1] // HEAD):
        cols = slice(h * HEAD, (h + 1) * HEAD)
        scores = lax.dot_general(
            q_ref[0, :, cols], keyed[:, cols], (((1,), (1,)), ((), ())),
            preferred_element_type=jnp.float32,
        )
        scores = jnp.where(valid, scores, -1e30)
        peak = jnp.max(scores, axis=-1, keepdims=True)
        raised = jnp.where(valid, jnp.exp(scores - peak), 0.0)
        weights = (raised * (1.0 / jnp.sum(raised, axis=-1, keepdims=True))).astype(jnp.bfloat16)
        o_ref[0, :, cols] = jnp.dot(
            weights, valued[:, cols], preferred_element_type=jnp.float32
        ).astype(jnp.bfloat16)


def attend(counts, shifted, all_rows, w_key, w_value, queries):
    questions, asked, cols = queries.shape
    total, width = all_rows.shape
    step = min(cols, 8 * HEAD)
    while cols % step:
        step -= HEAD
    return pl.pallas_call(
        attend_kernel,
        out_shape=jax.ShapeDtypeStruct(queries.shape, jnp.bfloat16),
        grid_spec=pltpu.PrefetchScalarGridSpec(
            num_scalar_prefetch=1,
            grid=(cols // step, questions),
            in_specs=[
                pl.BlockSpec((1, total), lambda c, q, s: (0, 0)),
                pl.BlockSpec((total, width), lambda c, q, s: (0, 0)),
                pl.BlockSpec((width, step), lambda c, q, s: (0, c)),
                pl.BlockSpec((width, step), lambda c, q, s: (0, c)),
                pl.BlockSpec((1, asked, step), lambda c, q, s: (q, 0, c)),
            ],
            out_specs=pl.BlockSpec((1, asked, step), lambda c, q, s: (q, 0, c)),
            scratch_shapes=[pltpu.VMEM((questions, SLOTS, width), jnp.bfloat16)],
        ),
        compiler_params=pltpu.CompilerParams(vmem_limit_bytes=56 * 1024 * 1024),
        name="attend",
    )(counts, shifted, all_rows, w_key, w_value, queries)


def per_device(devices, passages, gain, w_in, w_out, w_key, w_value, queries, ids, counts):
    outer = devices // INNER
    all_rows = encode(passages, gain, w_in, w_out, outer)
    slot_total = counts.shape[0] * SLOTS
    shifted = (ids - lax.axis_index("pass") * slot_total)[None, :]
    return attend(counts, shifted, all_rows, w_key, w_value, queries)


def solution(mesh):
    placed = (
        P(("groups", "pass", "mp"), None),
        P(),
        P(None, "mp"),
        P("mp", None),
        P(None, "mp"),
        P(None, "mp"),
        P(("groups", "pass"), None, "mp"),
        P("groups"),
        P(("groups", "pass")),
    )
    return jax.shard_map(
        functools.partial(per_device, mesh.shape["mp"]),
        mesh=mesh,
        in_specs=placed,
        out_specs=P(("groups", "pass"), None, "mp"),
        check_vma=False,
    )
```

time: 227 us -> 166 us (0.73)
  the two profiles are of different devices: /device:TPU:17 before, /device:TPU:0 now
where the time goes in v2:
time: 166 us
  Pallas kernels  165 us (99%)
    pallas_call x1, Pallas kernels, encode(): pl.pallas_call(functools.partial(encode_kernel, outer, rows, chunk), out_...  109 us
    pallas_call x1, Pallas kernels, attend(): pl.pallas_call(attend_kernel, out_shape=jax.ShapeDtypeStruct(queries.shap...  56.1 us

profile of v2, /device:TPU:0, one launch (start us, length us, event | category | flops | bytes accessed | tf_op | source)
XLA Modules:
  0.0 166.0 jit_solution(18091601905512268730)
XLA Ops:
  0.0 1.3 broadcast_subtract_fusion
  1.3 108.6 %encode.1.rows_ref = bf16[2048,1024]{1,0:T(8,128)(2,1)} custom-call(bf16[128,1024]{1,0:T(8,128)(2,1)} %own_ref.1, f32[1,1024]{1,0:T(1,128)} %bitcast.3, bf16[1024,8192]{1,0:T(8,128)(2,1)} %w_in_ref.1, bf16[8192,1024]{1,0:T(8,128)(2,1)} %w_out_ref.1), custom_call_target="tpu_custom_call" | custom-call | tf_op jit(solution)/shard_map/encode/pallas_call | solution.py:194
  109.9 56.1 %attend.1 = bf16[8,256,2048]{2,1,0:T(8,128)(2,1)} custom-call(s32[8]{0:T(128)} %counts_ref.1, s32[1,2048]{1,0:T(1,128)} %bitcast.2, bf16[2048,1024]{1,0:T(8,128)(2,1)} %encode.1.rows_ref, bf16[1024,2048]{1,0:T(8,128)(2,1)} %wk_ref.1, bf16[1024,2048]{1,0:T(8,128)(2,1)} %wv_ref.1, bf16[8,256,2048]{2,1,0:T(8,128)(2,1)} %q_ref.1), custom_call_target="tpu_custom_call" | custom-call | tf_op jit(solution)/shard_map/attend/pallas_call | solution.py:259

commit v3 on v2

--- a/solution.py
+++ b/solution.py
@@ -12,6 +12,7 @@
 SLOTS = 256
 MESH = pl.DeviceIdType.MESH
 INNER = 2
+ALIGN = 16
 
 
 def greet(targets):
@@ -151,26 +152,60 @@
     def block(pp, zz, yy):
         return out_ref.at[pl.ds(pl.multiple_of(pp * n * rows + start(zz, yy), rows), rows)]
 
-    mine = block(p, z, y)
-    sent = [push(mine, mine, ys.at[0], yr.at[0], partner)]
-    for k in range(outer - 1):
-        sent.append(push(mine, mine, zs.at[k], zr.at[k], {"mp": ahead[k] * INNER + y}))
-    sent.append(push(mine, mine, ps.at[0], pr.at[0], twin))
-    for k in range(1, outer):
-        arrived = block(p, behind[k - 1], y)
-        landed(arrived, zs.at[k - 1], zr.at[k - 1], partner)
-        sent.append(push(arrived, arrived, ys.at[k], yr.at[k], partner))
-        sent.append(push(arrived, arrived, ps.at[k], pr.at[k], twin))
+    def spread(zz):
+        here = block(p, zz, y)
+        push(here, here, ys.at[zz], yr.at[zz], partner)
+        push(here, here, ps.at[zz * INNER + y], pr.at[zz * INNER + y], twin)
+
+    def relay(zz, s, side, on, keep):
+        @pl.when(keep)
+        def _():
+            here = block(p, zz, y)
+            if s > 0:
+                landed(here, zs.at[side, s - 1], zr.at[side, s - 1], partner)
+            following = z + 1 if side == 0 else z - 1
+
+            @pl.when(on)
+            def _():
+                push(here, here, zs.at[side, s], zr.at[side, s], {"mp": following * INNER + y})
+
+            if s > 0:
+                spread(zz)
+
+    upward, downward = z < outer - 1, z > 0
+    for s in range(outer):
+        relay(z - s, s, 0, upward, z - s >= 0)
+        relay(z + s, s, 1, downward, z + s < outer)
+        if s == 0:
+            spread(z)
+
+    def cross(zz, keep):
+        @pl.when(keep)
+        def _():
+            here = block(p, zz, 1 - y)
+            landed(here, ys.at[zz], yr.at[zz], partner)
+            at = zz * INNER + 1 - y
+            push(here, here, ps.at[at], pr.at[at], twin)
+
+    cross(z, z >= 0)
+    for s in range(1, outer):
+        cross(z - s, z - s >= 0)
+        cross(z + s, z + s < outer)
+    for k in range(n):
+        landed(block(1 - p, k // INNER, k % INNER), ps.at[k], pr.at[k], twin)
+    for k in range(n):
+        gone(block(p, z, y), ps.at[k], pr.at[k], twin)
     for k in range(outer):
-        arrived = block(p, z if k == 0 else behind[k - 1], 1 - y)
-        landed(arrived, ys.at[k], yr.at[k], partner)
-        sent.append(push(arrived, arrived, ps.at[outer + k], pr.at[outer + k], twin))
-    for k in range(2 * outer):
-        kk = k % outer
-        arrived = block(1 - p, z if kk == 0 else behind[kk - 1], y if k < outer else 1 - y)
-        landed(arrived, ps.at[k], pr.at[k], twin)
-    for copy in sent:
-        copy.wait_send()
+        gone(block(p, z, y), ys.at[k], yr.at[k], partner)
+
+        @pl.when(upward & (z - k >= 0))
+        def _():
+            gone(block(p, z, y), zs.at[0, k], zr.at[0, k], partner)
+
+        @pl.when(downward & (z + k < outer))
+        def _():
+            gone(block(p, z, y), zs.at[1, k], zr.at[1, k], partner)
+
     for k in range(outer):
         gone(held(z, y), gys.at[k], gyr.at[k], partner)
         gone(from_y.at[k], rys.at[k], ryr.at[k], partner)
@@ -209,8 +244,8 @@
             dma((chunks,)), dma((chunks,)), dma,
             dma((outer - 1,)), dma((outer - 1,)), dma((outer,)), dma((outer,)),
             dma((outer,)), dma((outer,)), dma((outer - 1,)), dma((outer - 1,)),
-            dma((outer - 1,)), dma((outer - 1,)), dma((outer,)), dma((outer,)),
-            dma((2 * outer,)), dma((2 * outer,)),
+            dma((2, outer)), dma((2, outer)), dma((outer,)), dma((outer,)),
+            dma((n,)), dma((n,)),
         ],
         compiler_params=pltpu.CompilerParams(
             collective_id=0, has_side_effects=True, vmem_limit_bytes=60 * 1024 * 1024
@@ -219,35 +254,79 @@
     )(passages, gain[None, :], w_in, w_out)
 
 
-def attend_kernel(counts_ref, ids_ref, rows_ref, wk_ref, wv_ref, q_ref, o_ref, slot_ref):
+def attend_kernel(
+    counts_ref, ids_ref, rows_ref, wk_ref, wv_ref, q_ref, o_ref, slot_ref, key_ref, value_ref
+):
     q = pl.program_id(1)
-
-    @pl.when(pl.program_id(0) == 0)
+    first = pl.program_id(0) == 0
+    questions = counts_ref.shape[0]
+    offset, own_offset = [jnp.int32(0)], jnp.int32(0)
+    for j in range(questions):
+        room = (counts_ref[j] + ALIGN - 1) // ALIGN * ALIGN
+        own_offset += jnp.where(j < q, room, 0)
+        offset.append(offset[-1] + room)
+    own_offset = pl.multiple_of(own_offset, ALIGN)
+
+    @pl.when(q == 0)
     def _():
-        total = ids_ref.shape[1]
-        slot_id = lax.broadcasted_iota(jnp.int32, (SLOTS, total), 0) + q * SLOTS
-        named = jnp.where(slot_id == ids_ref[...], 1.0, 0.0).astype(jnp.bfloat16)
-        slot_ref[q] = jnp.dot(
-            named, rows_ref[...], preferred_element_type=jnp.float32
-        ).astype(jnp.bfloat16)
-
-    slots = slot_ref[q]
-    keyed = jnp.dot(slots, wk_ref[...], preferred_element_type=jnp.float32).astype(jnp.bfloat16)
-    valued = jnp.dot(slots, wv_ref[...], preferred_element_type=jnp.float32).astype(jnp.bfloat16)
-    valid = lax.broadcasted_iota(jnp.int32, (QUERIES, SLOTS), 1) < counts_ref[q]
-    for h in range(wk_ref.shape[1] // HEAD):
-        cols = slice(h * HEAD, (h + 1) * HEAD)
-        scores = lax.dot_general(
-            q_ref[0, :, cols], keyed[:, cols], (((1,), (1,)), ((), ())),
-            preferred_element_type=jnp.float32,
-        )
-        scores = jnp.where(valid, scores, -1e30)
-        peak = jnp.max(scores, axis=-1, keepdims=True)
-        raised = jnp.where(valid, jnp.exp(scores - peak), 0.0)
-        weights = (raised * (1.0 / jnp.sum(raised, axis=-1, keepdims=True))).astype(jnp.bfloat16)
-        o_ref[0, :, cols] = jnp.dot(
-            weights, valued[:, cols], preferred_element_type=jnp.float32
-        ).astype(jnp.bfloat16)
+        tiles = (offset[questions] + SLOTS - 1) // SLOTS
+
+        def tile(t, carry):
+            here = pl.ds(pl.multiple_of(t * SLOTS, SLOTS), SLOTS)
+
+            @pl.when(first)
+            def _():
+                ids = ids_ref[...]
+                packed = jnp.full_like(ids, -1)
+                for j in range(questions):
+                    mine = (ids >= j * SLOTS) & (ids < (j + 1) * SLOTS)
+                    packed = jnp.where(mine, ids - j * SLOTS + offset[j], packed)
+                line = lax.broadcasted_iota(jnp.int32, (SLOTS, ids.shape[1]), 0) + t * SLOTS
+                named = jnp.where(line == packed, 1.0, 0.0).astype(jnp.bfloat16)
+                slot_ref[here, :] = jnp.dot(
+                    named, rows_ref[...], preferred_element_type=jnp.float32
+                ).astype(jnp.bfloat16)
+
+            slots = slot_ref[here, :]
+            key_ref[here, :] = jnp.dot(
+                slots, wk_ref[...], preferred_element_type=jnp.float32
+            ).astype(jnp.bfloat16)
+            value_ref[here, :] = jnp.dot(
+                slots, wv_ref[...], preferred_element_type=jnp.float32
+            ).astype(jnp.bfloat16)
+            return carry
+
+        lax.fori_loop(0, tiles, tile, 0)
+        tail = pl.ds(pl.multiple_of(tiles * SLOTS, SLOTS), SLOTS)
+        value_ref[tail, :] = jnp.zeros((SLOTS, value_ref.shape[1]), jnp.bfloat16)
+
+    def mix(width):
+        valid = lax.broadcasted_iota(jnp.int32, (QUERIES, width), 1) < counts_ref[q]
+        for h in range(wk_ref.shape[1] // HEAD):
+            cols = slice(h * HEAD, (h + 1) * HEAD)
+            scores = lax.dot_general(
+                q_ref[0, :, cols], key_ref[pl.ds(own_offset, width), cols],
+                (((1,), (1,)), ((), ())), preferred_element_type=jnp.float32,
+            )
+            scores = jnp.where(valid, scores, -1e30)
+            peak = jnp.max(scores, axis=-1, keepdims=True)
+            raised = jnp.where(valid, jnp.exp(scores - peak), 0.0)
+            share = 1.0 / jnp.sum(raised, axis=-1, keepdims=True)
+            o_ref[0, :, cols] = jnp.dot(
+                (raised * share).astype(jnp.bfloat16),
+                value_ref[pl.ds(own_offset, width), cols],
+                preferred_element_type=jnp.float32,
+            ).astype(jnp.bfloat16)
+
+    few = counts_ref[q] <= SLOTS // 2
+
+    @pl.when(few)
+    def _():
+        mix(SLOTS // 2)
+
+    @pl.when(jnp.logical_not(few))
+    def _():
+        mix(SLOTS)
 
 
 def attend(counts, shifted, all_rows, w_key, w_value, queries):
@@ -270,7 +349,11 @@
                 pl.BlockSpec((1, asked, step), lambda c, q, s: (q, 0, c)),
             ],
             out_specs=pl.BlockSpec((1, asked, step), lambda c, q, s: (q, 0, c)),
-            scratch_shapes=[pltpu.VMEM((questions, SLOTS, width), jnp.bfloat16)],
+            scratch_shapes=[
+                pltpu.VMEM((questions * SLOTS, width), jnp.bfloat16),
+                pltpu.VMEM((questions * SLOTS + SLOTS, step), jnp.bfloat16),
+                pltpu.VMEM((questions * SLOTS + SLOTS, step), jnp.bfloat16),
+            ],
         ),
         compiler_params=pltpu.CompilerParams(vmem_limit_bytes=56 * 1024 * 1024),
         name="attend",

time: 166 us -> 157 us (0.946)
  the two profiles are of different devices: /device:TPU:0 before, /device:TPU:1 now
where the time goes in v3:
time: 157 us
  Pallas kernels  155 us (99%)
    pallas_call x1, Pallas kernels, encode(): pl.pallas_call(functools.partial(encode_kernel, outer, rows, chunk), out_...  106 us
    pallas_call x1, Pallas kernels, attend(): pl.pallas_call(attend_kernel, out_shape=jax.ShapeDtypeStruct(queries.shap...  49 us

profile of v3, /device:TPU:1, one launch (start us, length us, event | category | flops | bytes accessed | tf_op | source)
XLA Modules:
  0.0 156.6 jit_solution(10014415515290394068)
XLA Ops:
  0.0 1.3 broadcast_subtract_fusion
  1.3 106.2 %encode.1.rows_ref = bf16[2048,1024]{1,0:T(8,128)(2,1)} custom-call(bf16[128,1024]{1,0:T(8,128)(2,1)} %own_ref.1, f32[1,1024]{1,0:T(1,128)} %bitcast.3, bf16[1024,8192]{1,0:T(8,128)(2,1)} %w_in_ref.1, bf16[8192,1024]{1,0:T(8,128)(2,1)} %w_out_ref.1), custom_call_target="tpu_custom_call" | custom-call | tf_op jit(solution)/shard_map/encode/pallas_call | solution.py:229
  107.5 49.0 %attend.1 = bf16[8,256,2048]{2,1,0:T(8,128)(2,1)} custom-call(s32[8]{0:T(128)} %counts_ref.1, s32[1,2048]{1,0:T(1,128)} %bitcast.2, bf16[2048,1024]{1,0:T(8,128)(2,1)} %encode.1.rows_ref, bf16[1024,2048]{1,0:T(8,128)(2,1)} %wk_ref.1, bf16[1024,2048]{1,0:T(8,128)(2,1)} %wv_ref.1, bf16[8,256,2048]{2,1,0:T(8,128)(2,1)} %q_ref.1), custom_call_target="tpu_custom_call" | custom-call | tf_op jit(solution)/shard_map/attend/pallas_call | solution.py:338

commit v4 on v3

--- a/solution.py
+++ b/solution.py
@@ -13,6 +13,7 @@
 MESH = pl.DeviceIdType.MESH
 INNER = 2
 ALIGN = 16
+AHEAD = 3
 
 
 def greet(targets):
@@ -62,6 +63,8 @@
     z, y, partner, ahead, behind = place(outer, INNER)
     n = outer * INNER
     chunks = w_in_here.shape[0]
+    cuts = ryr.shape[1]
+    cut = rows // cuts
     p = lax.axis_index("pass")
     twin = {"pass": 1 - p}
 
@@ -73,7 +76,7 @@
         cols = pl.ds(pl.multiple_of(c * chunk, chunk), chunk)
         return pltpu.make_async_copy(w_out_ref.at[cols, :], w_out_here.at[c], out_sem.at[c])
 
-    for c in range(chunks):
+    for c in range(min(AHEAD, chunks)):
         load_in(c).start()
         load_out(c).start()
     greet([partner, twin] + [{"mp": zz * INNER + y} for zz in ahead])
@@ -92,14 +95,16 @@
     local.wait()
 
     def add_pair(k):
-        landed(from_y.at[k], rys.at[k], ryr.at[k], partner)
-        here = parts[k, pl.ds(pl.multiple_of(y * rows, rows), rows), :]
-        summed[k - 1] = (
-            here.astype(jnp.float32) + from_y[k].astype(jnp.float32)
-        ).astype(jnp.bfloat16)
         owner = (z + outer - k) % outer
-        push(summed.at[k - 1], from_z.at[k - 1], rzs.at[k - 1], rzr.at[k - 1],
-             {"mp": owner * INNER + y})
+        for i in range(cuts):
+            at = pl.ds(i * cut, cut)
+            landed(from_y.at[k, at], rys.at[k, i], ryr.at[k, i], partner)
+            here = parts[k, pl.ds(pl.multiple_of(y * rows + i * cut, cut), cut), :]
+            summed[k - 1, at, :] = (
+                here.astype(jnp.float32) + from_y[k, at, :].astype(jnp.float32)
+            ).astype(jnp.bfloat16)
+            push(summed.at[k - 1, at], from_z.at[k - 1, at], rzs.at[k - 1, i],
+                 rzr.at[k - 1, i], {"mp": owner * INNER + y})
 
     def group(k, carry):
         zz = (z + outer - k) % outer
@@ -112,6 +117,11 @@
         def piece(c, carry):
             @pl.when(k == 0)
             def _():
+                @pl.when(c + AHEAD < chunks)
+                def _():
+                    load_in(c + AHEAD).start()
+                    load_out(c + AHEAD).start()
+
                 load_in(c).wait()
                 load_out(c).wait()
 
@@ -134,84 +144,99 @@
 
         lax.fori_loop(0, chunks, piece, 0)
         parts[k] = total[...].astype(jnp.bfloat16)
-        push(parts.at[k, pl.ds(pl.multiple_of((1 - y) * rows, rows), rows)], from_y.at[k],
-             rys.at[k], ryr.at[k], partner)
+        for i in range(cuts):
+            away = pl.ds(pl.multiple_of((1 - y) * rows + i * cut, cut), cut)
+            push(parts.at[k, away], from_y.at[k, pl.ds(i * cut, cut)], rys.at[k, i],
+                 ryr.at[k, i], partner)
         return carry
 
     lax.fori_loop(0, outer, group, 0)
     add_pair(outer - 1)
-    landed(from_y.at[0], rys.at[0], ryr.at[0], partner)
-    mine = pl.ds(pl.multiple_of(y * rows, rows), rows)
-    ffn = parts[0, mine, :].astype(jnp.float32) + from_y[0].astype(jnp.float32)
-    for k in range(outer - 1):
-        landed(from_z.at[k], rzs.at[k], rzr.at[k], partner)
-        ffn += from_z[k].astype(jnp.float32)
-    own = pl.multiple_of(p * n * rows + start(z, y), rows)
-    out_ref[pl.ds(own, rows), :] = (own_ref[...].astype(jnp.float32) + ffn).astype(jnp.bfloat16)
-
-    def block(pp, zz, yy):
-        return out_ref.at[pl.ds(pl.multiple_of(pp * n * rows + start(zz, yy), rows), rows)]
-
-    def spread(zz):
-        here = block(p, zz, y)
-        push(here, here, ys.at[zz], yr.at[zz], partner)
-        push(here, here, ps.at[zz * INNER + y], pr.at[zz * INNER + y], twin)
-
-    def relay(zz, s, side, on, keep):
+
+    def block(pp, zz, yy, i):
+        first = pp * n * rows + start(zz, yy) + i * cut
+        return out_ref.at[pl.ds(pl.multiple_of(first, cut), cut)]
+
+    def spread(zz, i):
+        here = block(p, zz, y, i)
+        at = zz * INNER + y
+        push(here, here, ys.at[zz, i], yr.at[zz, i], partner)
+        push(here, here, ps.at[at, i], pr.at[at, i], twin)
+
+    def relay(zz, s, side, on, keep, i):
         @pl.when(keep)
         def _():
-            here = block(p, zz, y)
+            here = block(p, zz, y, i)
             if s > 0:
-                landed(here, zs.at[side, s - 1], zr.at[side, s - 1], partner)
+                landed(here, zs.at[side, s - 1, i], zr.at[side, s - 1, i], partner)
             following = z + 1 if side == 0 else z - 1
 
             @pl.when(on)
             def _():
-                push(here, here, zs.at[side, s], zr.at[side, s], {"mp": following * INNER + y})
+                push(here, here, zs.at[side, s, i], zr.at[side, s, i],
+                     {"mp": following * INNER + y})
 
             if s > 0:
-                spread(zz)
+                spread(zz, i)
 
     upward, downward = z < outer - 1, z > 0
-    for s in range(outer):
-        relay(z - s, s, 0, upward, z - s >= 0)
-        relay(z + s, s, 1, downward, z + s < outer)
-        if s == 0:
-            spread(z)
-
-    def cross(zz, keep):
+    for i in range(cuts):
+        at = pl.ds(i * cut, cut)
+        landed(from_y.at[0, at], rys.at[0, i], ryr.at[0, i], partner)
+        mine = pl.ds(pl.multiple_of(y * rows + i * cut, cut), cut)
+        ffn = parts[0, mine, :].astype(jnp.float32) + from_y[0, at, :].astype(jnp.float32)
+        for k in range(outer - 1):
+            landed(from_z.at[k, at], rzs.at[k, i], rzr.at[k, i], partner)
+            ffn += from_z[k, at, :].astype(jnp.float32)
+        own = pl.multiple_of(p * n * rows + start(z, y) + i * cut, cut)
+        out_ref[pl.ds(own, cut), :] = (
+            own_ref[at, :].astype(jnp.float32) + ffn
+        ).astype(jnp.bfloat16)
+        relay(z, 0, 0, upward, z >= 0, i)
+        relay(z, 0, 1, downward, z >= 0, i)
+        spread(z, i)
+    for s in range(1, outer):
+        for i in range(cuts):
+            relay(z - s, s, 0, upward, z - s >= 0, i)
+            relay(z + s, s, 1, downward, z + s < outer, i)
+
+    def cross(zz, keep, i):
         @pl.when(keep)
         def _():
-            here = block(p, zz, 1 - y)
-            landed(here, ys.at[zz], yr.at[zz], partner)
+            here = block(p, zz, 1 - y, i)
+            landed(here, ys.at[zz, i], yr.at[zz, i], partner)
             at = zz * INNER + 1 - y
-            push(here, here, ps.at[at], pr.at[at], twin)
-
-    cross(z, z >= 0)
+            push(here, here, ps.at[at, i], pr.at[at, i], twin)
+
+    for i in range(cuts):
+        cross(z, z >= 0, i)
     for s in range(1, outer):
-        cross(z - s, z - s >= 0)
-        cross(z + s, z + s < outer)
-    for k in range(n):
-        landed(block(1 - p, k // INNER, k % INNER), ps.at[k], pr.at[k], twin)
-    for k in range(n):
-        gone(block(p, z, y), ps.at[k], pr.at[k], twin)
-    for k in range(outer):
-        gone(block(p, z, y), ys.at[k], yr.at[k], partner)
-
-        @pl.when(upward & (z - k >= 0))
-        def _():
-            gone(block(p, z, y), zs.at[0, k], zr.at[0, k], partner)
-
-        @pl.when(downward & (z + k < outer))
-        def _():
-            gone(block(p, z, y), zs.at[1, k], zr.at[1, k], partner)
-
+        for i in range(cuts):
+            cross(z - s, z - s >= 0, i)
+            cross(z + s, z + s < outer, i)
+    for i in range(cuts):
+        some = block(p, z, y, i)
+        for k in range(n):
+            landed(block(1 - p, k // INNER, k % INNER, i), ps.at[k, i], pr.at[k, i], twin)
+            gone(some, ps.at[k, i], pr.at[k, i], twin)
+        for k in range(outer):
+            gone(some, ys.at[k, i], yr.at[k, i], partner)
+            gone(some, rys.at[k, i], ryr.at[k, i], partner)
+
+            @pl.when(upward & (z - k >= 0))
+            def _():
+                gone(some, zs.at[0, k, i], zr.at[0, k, i], partner)
+
+            @pl.when(downward & (z + k < outer))
+            def _():
+                gone(some, zs.at[1, k, i], zr.at[1, k, i], partner)
+
+        for k in range(outer - 1):
+            gone(some, rzs.at[k, i], rzr.at[k, i], partner)
     for k in range(outer):
         gone(held(z, y), gys.at[k], gyr.at[k], partner)
-        gone(from_y.at[k], rys.at[k], ryr.at[k], partner)
     for k in range(outer - 1):
         gone(held(z, y), gzs.at[k], gzr.at[k], partner)
-        gone(summed.at[k], rzs.at[k], rzr.at[k], partner)
 
 
 def encode(passages, gain, w_in, w_out, outer):
@@ -222,6 +247,7 @@
     while units % chunk:
         chunk -= 128
     chunks = units // chunk
+    cuts = 2 if rows % (2 * ALIGN) == 0 else 1
     dma = pltpu.SemaphoreType.DMA
     vmem = pl.BlockSpec(memory_space=pltpu.VMEM)
     hbm = pl.BlockSpec(memory_space=pl.ANY)
@@ -243,9 +269,9 @@
             pltpu.VMEM((outer - 1, rows, width), bf16),
             dma((chunks,)), dma((chunks,)), dma,
             dma((outer - 1,)), dma((outer - 1,)), dma((outer,)), dma((outer,)),
-            dma((outer,)), dma((outer,)), dma((outer - 1,)), dma((outer - 1,)),
-            dma((2, outer)), dma((2, outer)), dma((outer,)), dma((outer,)),
-            dma((n,)), dma((n,)),
+            dma((outer, cuts)), dma((outer, cuts)), dma((outer - 1, cuts)), dma((outer - 1, cuts)),
+            dma((2, outer, cuts)), dma((2, outer, cuts)), dma((outer, cuts)), dma((outer, cuts)),
+            dma((n, cuts)), dma((n, cuts)),
         ],
         compiler_params=pltpu.CompilerParams(
             collective_id=0, has_side_effects=True, vmem_limit_bytes=60 * 1024 * 1024
@@ -310,7 +336,7 @@
             )
             scores = jnp.where(valid, scores, -1e30)
             peak = jnp.max(scores, axis=-1, keepdims=True)
-            raised = jnp.where(valid, jnp.exp(scores - peak), 0.0)
+            raised = jnp.exp(scores - peak)
             share = 1.0 / jnp.sum(raised, axis=-1, keepdims=True)
             o_ref[0, :, cols] = jnp.dot(
                 (raised * share).astype(jnp.bfloat16),

time: 157 us -> 154 us (0.981)
  the two profiles are of different devices: /device:TPU:1 before, /device:TPU:0 now
where the time goes in v4:
time: 154 us; the launch traced here: 153 us
  Pallas kernels  152 us (99%)
    pallas_call x1, Pallas kernels, encode(): pl.pallas_call(functools.partial(encode_kernel, outer, rows, chunk), out_...  103 us
    pallas_call x1, Pallas kernels, attend(): pl.pallas_call(attend_kernel, out_shape=jax.ShapeDtypeStruct(queries.shap...  49 us

profile of v4, /device:TPU:0, one launch (start us, length us, event | category | flops | bytes accessed | tf_op | source)
XLA Modules:
  0.0 153.4 jit_solution(15902900768870476349)
XLA Ops:
  0.0 1.3 broadcast_subtract_fusion
  1.3 103.1 %encode.1.rows_ref = bf16[2048,1024]{1,0:T(8,128)(2,1)} custom-call(bf16[128,1024]{1,0:T(8,128)(2,1)} %own_ref.1, f32[1,1024]{1,0:T(1,128)} %bitcast.3, bf16[1024,8192]{1,0:T(8,128)(2,1)} %w_in_ref.1, bf16[8192,1024]{1,0:T(8,128)(2,1)} %w_out_ref.1), custom_call_target="tpu_custom_call" | custom-call | tf_op jit(solution)/shard_map/encode/pallas_call | solution.py:255
  104.4 49.0 %attend.1 = bf16[8,256,2048]{2,1,0:T(8,128)(2,1)} custom-call(s32[8]{0:T(128)} %counts_ref.1, s32[1,2048]{1,0:T(1,128)} %bitcast.2, bf16[2048,1024]{1,0:T(8,128)(2,1)} %encode.1.rows_ref, bf16[1024,2048]{1,0:T(8,128)(2,1)} %wk_ref.1, bf16[1024,2048]{1,0:T(8,128)(2,1)} %wv_ref.1, bf16[8,256,2048]{2,1,0:T(8,128)(2,1)} %q_ref.1), custom_call_target="tpu_custom_call" | custom-call | tf_op jit(solution)/shard_map/attend/pallas_call | solution.py:364
